TPU v7x, 32 devices: a whole 2x2x4 slice. The times are simulated.
32 devices in a mesh: row: 8 (over z, y), col: 4 (over x, core).
Axes of the slice: x: 2, y: 2, z: 4, core: 2. Of those that a mesh axis runs over, the one named last changes fastest.
Arguments:
- ancestor_inverse: float32 [12288, 12288], P('row', 'col'), may hold values from -5 to 320, as said below
- panel_one: float32 [12288, 256], P(('row', 'col')), may hold values from -0.015625 to 0.015625
- struct_one: int32 [10752], replicated, may hold values from 0 to 12287, as said below
- lower_one: float32 [256, 256], replicated, may hold values from -1 to 2, as said below
- panel_two: float32 [12288, 256], P(('row', 'col')), may hold values from -0.015625 to 0.015625
- struct_two: int32 [9216], replicated, may hold values from 0 to 12287, as said below
- panel_above: float32 [256, 256], replicated, may hold values from -0.375 to 0.375
- lower_two: float32 [256, 256], replicated, may hold values from -1 to 2, as said below
- tile_owner: int32 [192, 1], P(('col', 'row')), may hold values from 0 to 3; in each aligned block of 6 rows (0 to 5, 6 to 11, ...) at most 2 rows name the same one
Outputs:
- inverse_one: float32 [12288, 256], P(('col', 'row'))
- diag_one: float32 [256, 256], replicated
- cross_two: float32 [256, 256], replicated
- diag_two: float32 [256, 256], replicated
- delivered: float32 [256, 64, 256], P(('row', 'col'))
Inputs may be any that keep to these rules, and one draw needn't show every extreme that they name: ancestor_inverse is exactly symmetric and positive definite. `struct_one`: 10752 distinct row numbers of the ancestor block. `struct_two`: 9216 distinct entries of struct_one. `lower_one`: lower triangular with a positive diagonal. `lower_two`: lower triangular with a positive diagonal. `tile_owner`: within each aligned block of 6 entries (the tiles of one device) no value appears more than 2 times; in some block a value appears exactly 2 times.
All inputs are finite; a program needn't handle non-finite values.
Results may differ from a plain program's by a relative error of at most 0.00007.
Values sent between devices are 32-bit elements; how exact they have to be, the bound alone decides.
A program may use at most 64 MiB of HBM per device.

v0:
```python
import jax
import jax.numpy as jnp
from jax import lax
from jax.sharding import PartitionSpec as P

CAP = 2


def matmul(left, right):
    return jnp.dot(left, right, precision=lax.Precision.HIGHEST, preferred_element_type=jnp.float32)


def contract_rows(left, right, precision=lax.Precision.HIGHEST):
    return lax.dot_general(
        left,
        right,
        (((0,), (0,)), ((), ())),
        precision=precision,
        preferred_element_type=jnp.float32,
    )


def row_mask(struct, count):
    lanes = 128
    high = struct // lanes
    low = struct % lanes
    high_hot = (jnp.arange(count // lanes, dtype=jnp.int32)[:, None] == high[None, :]).astype(
        jnp.bfloat16
    )
    low_hot = (jnp.arange(lanes, dtype=jnp.int32)[:, None] == low[None, :]).astype(jnp.bfloat16)
    counts = lax.dot_general(
        high_hot, low_hot, (((1,), (1,)), ((), ())), preferred_element_type=jnp.float32
    )
    return (counts > 0.5).astype(jnp.float32).reshape(count)


def deliver(values, tile_owner, col_count):
    tile_count = tile_owner.shape[0]
    tile_rows = values.shape[0] // tile_count
    all_tiles = values.reshape(tile_count, tile_rows, values.shape[1])
    owner_col = tile_owner[:, 0]
    col_ids = jnp.arange(col_count, dtype=jnp.int32)
    onehot = (owner_col[:, None] == col_ids[None, :]).astype(jnp.int32)
    tile_rank = jnp.sum((jnp.cumsum(onehot, axis=0) - onehot) * onehot, axis=1)
    slot_index = jnp.arange(CAP, dtype=jnp.int32)
    select = (
        (owner_col[None, None, :] == col_ids[:, None, None])
        & (tile_rank[None, None, :] == slot_index[None, :, None])
    ).astype(jnp.float32)
    outgoing = jnp.einsum("cks,srb->ckrb", select, all_tiles, precision=lax.Precision.HIGHEST)
    incoming = lax.all_to_all(outgoing, "col", split_axis=0, concat_axis=0, tiled=True)
    return incoming.reshape(col_count * CAP, tile_rows, values.shape[1])


def local(
    ancestor_inverse,
    panel_one,
    struct_one,
    lower_one,
    panel_two,
    struct_two,
    panel_above,
    lower_two,
    tile_owner,
):
    row_count = lax.axis_size("row")
    col_count = lax.axis_size("col")
    row_index = lax.axis_index("row")
    col_index = lax.axis_index("col")
    local_rows = panel_one.shape[0]
    order = local_rows * row_count * col_count
    width = panel_one.shape[1]
    mask_one = row_mask(struct_one, order)
    mask_two = row_mask(struct_two, order)
    panel_start = (row_index * col_count + col_index) * local_rows
    result_start = (col_index * row_count + row_index) * local_rows
    local_one = panel_one * lax.dynamic_slice_in_dim(mask_one, panel_start, local_rows)[:, None]
    local_two = panel_two * lax.dynamic_slice_in_dim(mask_two, panel_start, local_rows)[:, None]
    result_mask_one = lax.dynamic_slice_in_dim(mask_one, result_start, local_rows)[:, None]
    result_mask_two = lax.dynamic_slice_in_dim(mask_two, result_start, local_rows)[:, None]
    both = jnp.concatenate([local_one, local_two], axis=1)
    gathered = lax.all_gather(both, "col", axis=0, tiled=True)
    moves = [(f, f % row_count * col_count + f // row_count) for f in range(row_count * col_count)]
    resident = lax.ppermute(both, ("row", "col"), moves)
    product = lax.psum_scatter(
        contract_rows(ancestor_inverse, gathered, lax.Precision.HIGH),
        "row",
        scatter_dimension=0,
        tiled=True,
    )
    resident_one = resident[:, :width]
    resident_two = resident[:, width:]
    inverse_one = -product[:, :width] * result_mask_one
    inverse_two = -(product[:, width:] + matmul(inverse_one, panel_above)) * result_mask_two
    sums = lax.psum(
        jnp.concatenate(
            [
                contract_rows(resident_one, inverse_one),
                contract_rows(inverse_one, resident_two),
                contract_rows(resident_two, inverse_two),
            ],
            axis=1,
        ),
        ("row", "col"),
    )
    gram_one = sums[:, :width]
    cross_sum = sums[:, width : 2 * width]
    gram_two = sums[:, 2 * width :]
    diag_one = matmul(lower_one.T, lower_one) - gram_one
    cross_two = -(cross_sum + matmul(diag_one, panel_above))
    diag_two = matmul(lower_two.T, lower_two) - gram_two - matmul(panel_above.T, cross_two)
    delivered = deliver(inverse_two, tile_owner, col_count)
    return (inverse_one, diag_one, cross_two, diag_two, delivered)


def solution(mesh):
    return jax.shard_map(
        local,
        mesh=mesh,
        in_specs=(
            P("row", "col"),
            P(("row", "col"), None),
            P(),
            P(),
            P(("row", "col"), None),
            P(),
            P(),
            P(),
            P(("col", "row"), None),
        ),
        out_specs=(P(("col", "row"), None), P(), P(), P(), P(("row", "col"), None, None)),
        check_vma=False,
    )
```

profile of v0, /device:TPU:0, one launch (start us, length us, event | category | flops | bytes accessed | tf_op | source)
XLA Modules:
  0.0 391.7 jit_solution(2987590773812136722)
XLA Ops:
  7.2 0.0 copy-start
  7.2 0.0 copy-start.6
  7.2 0.0 copy-start.7
  7.2 0.0 all-gather.2.cloned.1.call-start
  7.3 0.9 add_select_fusion.1
  8.2 0.8 add_select_fusion.3
  9.0 1.4 fusion.15
  10.4 1.3 fusion.12
  11.7 0.1 fusion.35
  11.8 0.0 copy-done.6
  11.8 0.1 broadcast_multiply_fusion
  11.9 0.0 copy-done.7
  11.9 0.1 broadcast_multiply_fusion.1
  12.0 1.0 pad_maximum_fusion
  13.0 0.0 all-gather.2.cloned.1.call-update
  13.0 0.0 reduce-scatter.2.cloned.1.call-start
  13.1 31.3 %all-gather.2.cloned.1.call-done = f32[1536,512]{1,0:T(8,128)} async-done(((f32[384,512]{1,0:T(8,128)}), f32[1536,512]{1,0:T(8,128)}) %all-gather.2.cloned.1.call-update) | async-done | bytes 3145744 | tf_op jit(solution)/shard_map/all_gather | solution.py:82
  44.4 22.2 %convolution_bitcast_fusion = f32[3072,512]{0,1:T(8,128)} fusion(f32[1536,512]{1,0:T(8,128)} %all-gather.2.cloned.1.call-done, f32[1536,3072]{1,0:T(8,128)} %param.9), kind=kOutput, calls=%fused_computation.2 | convolution fusion | flops 14495514624 | bytes 28311552 | tf_op jit(solution)/shard_map/dot_general | solution.py:14
  66.6 0.0 copy-start.1
  66.6 0.0 copy-start.8
  66.6 0.0 reduce-scatter.2.cloned.1.call-update
  66.6 1.1 copy-done.1
  67.7 0.7 collective-permute-start
  68.4 0.0 copy-done.8
  68.5 0.2 reduce_window_sum.11
  68.7 166.1 %reduce-scatter.2.cloned.1.call-done = f32[384,512]{0,1:T(8,128)} async-done(((f32[3072,512]{0,1:T(8,128)}), f32[384,512]{0,1:T(8,128)}) %reduce-scatter.2.cloned.1.call-update) | async-done | bytes 786448 | tf_op jit(solution)/shard_map/reduce_scatter | solution.py:85
  234.8 1.0 fusion.21
  235.8 0.0 copy-done
  235.9 1.6 fusion.7
  237.5 0.2 copy.44
  237.7 0.7 fusion.16
  238.3 0.0 copy-start.2
  238.4 0.9 copy.46
  239.2 3.5 all-to-all-start
  242.7 0.2 all-reduce.2.cloned.1.call-start
  243.0 0.0 collective-permute-done
  243.0 0.0 copy-start.3
  243.0 0.8 fusion.19
  243.8 0.6 fusion.24
  244.4 0.8 fusion.22
  245.2 1.0 pad_maximum_fusion.1
  246.2 0.0 all-reduce.2.cloned.1.call-update
  246.2 0.9 copy.47
  247.1 4.4 %all-to-all-done = f32[4,2,64,256]{3,2,1,0:T(8,128)S(1)} async-done(((f32[4,2,64,256]{3,2,1,0:T(8,128)}), f32[4,2,64,256]{3,2,1,0:T(8,128)S(1)}, u32[]{:S(2)}, u32[]{:S(2)}) %all-to-all-start) | async-done | bytes 524320 | tf_op jit(solution)/shard_map/all_to_all | solution.py:51
  251.5 126.9 %all-reduce.2.cloned.1.call-done = f32[256,768]{1,0:T(8,128)} async-done(((f32[256,768]{1,0:T(8,128)}), f32[256,768]{1,0:T(8,128)}) %all-reduce.2.cloned.1.call-update) | async-done | bytes 786448 | tf_op jit(solution)/shard_map/psum | solution.py:95
  378.4 0.0 copy-done.2
  378.4 1.5 convolution_subtract_fusion.1
  379.9 0.0 copy-start.4
  379.9 1.4 fusion.9
  381.4 0.0 copy-done.3
  381.4 0.0 copy-start.5
  381.4 1.6 convolution_subtract_fusion
  383.0 1.3 fusion.8
  384.3 0.8 copy.60
  385.1 0.0 copy-done.4
  385.1 0.0 copy-done.5
  (4 shorter events, 0.0 us)
Async XLA Ops:
  7.2 228.7 %copy-start = (f32[256,256]{1,0:T(8,128)S(1)}, f32[256,256]{1,0:T(8,128)}, u32[]{:S(2)}) copy-start(f32[256,256]{1,0:T(8,128)} %param.15) | copy-start | bytes 786436
  7.2 4.6 %copy-start.6 = (f32[384,256]{1,0:T(8,128)S(1)}, f32[384,256]{1,0:T(8,128)}, u32[]{:S(2)}) copy-start(f32[384,256]{1,0:T(8,128)} %param.13) | copy-start | bytes 1179652
  7.2 4.7 %copy-start.7 = (f32[384,256]{1,0:T(8,128)S(1)}, f32[384,256]{1,0:T(8,128)}, u32[]{:S(2)}) copy-start(f32[384,256]{1,0:T(8,128)} %param.10) | copy-start | bytes 1179652
  7.2 37.2 %all-gather.2.cloned.1.call-start = ((), (), s32[]{:S(2)}) async-start(), calls=%async_computation.2 | async-start | bytes 3932160 | tf_op jit(solution)/shard_map/all_gather | solution.py:82
  13.0 221.8 %reduce-scatter.2.cloned.1.call-start = ((), (), s32[]{:S(2)}) async-start(), calls=%async_computation.3 | async-start | bytes 7077888 | tf_op jit(solution)/shard_map/reduce_scatter | solution.py:85
  66.6 1.1 copy-start.1
  66.6 1.8 copy-start.8
  67.7 175.2 %collective-permute-start = (f32[384,512]{1,0:T(8,128)S(1)}, f32[384,512]{1,0:T(8,128)S(1)}, u32[]{:S(2)}, u32[]{:S(2)}) collective-permute-start(f32[384,512]{1,0:T(8,128)S(1)} %copy-done.1), channel_id=1, source_target_pairs={{0,0},{1,4},{2,8},{3,12},{4,16},{5,20},{6,24},{7,28},{8,1},{9,5},{... | collective-permute-start | bytes 2359304 | tf_op jit(solution)/shard_map/ppermute | solution.py:84
  238.3 140.0 %copy-start.2 = (f32[256,256]{1,0:T(8,128)S(1)}, f32[256,256]{1,0:T(8,128)}, u32[]{:S(2)}) copy-start(f32[256,256]{1,0:T(8,128)} %param.12) | copy-start | bytes 786436
  239.2 12.3 %all-to-all-start = ((f32[4,2,64,256]{3,2,1,0:T(8,128)}), f32[4,2,64,256]{3,2,1,0:T(8,128)S(1)}, u32[]{:S(2)}, u32[]{:S(2)}) async-start(f32[4,2,64,256]{3,2,1,0:T(8,128)} %copy.46), calls=%async_computation.1 | async-start | bytes 1048576 | tf_op jit(solution)/shard_map/all_to_all | solution.py:51
  242.7 135.6 %all-reduce.2.cloned.1.call-start = ((), (), s32[]{:S(2)}) async-start(), calls=%async_computation.4 | async-start | bytes 1572864 | tf_op jit(solution)/shard_map/psum | solution.py:95
  243.0 138.4 %copy-start.3 = (f32[256,256]{1,0:T(8,128)S(1)}, f32[256,256]{1,0:T(8,128)}, u32[]{:S(2)}) copy-start(f32[256,256]{1,0:T(8,128)} %param.16) | copy-start | bytes 786436
  379.9 5.2 %copy-start.4 = (f32[256,256]{1,0:T(8,128)}, f32[256,256]{1,0:T(8,128)S(1)}, u32[]{:S(2)}) copy-start(f32[256,256]{1,0:T(8,128)S(1)} %convolution_subtract_fusion.1) | copy-start | bytes 786436
  381.4 3.8 copy-start.5
Sparse Core Ops, SparseCore 0:
  13.2 31.2 all-gather.1
  66.7 168.0 reduce-scatter.1
  248.7 129.5 all-reduce.1
where the time goes:
time: 392 us
  waiting for transfers between devices  329 us (84%)
  matrix products  35.3 us (9%)
  between operations  14 us (4%)
  other arithmetic  5.13 us (1%)
  starting transfers between devices  4.47 us (1%)
  local copies, waits for them, and re-layouts  4 us (1%)
    reduce_scatter x1, waiting for transfers between devices, local(): lax.psum_scatter(contract_rows(ancestor_inverse, gathered, lax.Precision....  166 us
    psum x1, waiting for transfers between devices, local(): lax.psum(jnp.concatenate([contract_rows(resident_one, inverse_one), contr...  127 us
    all_gather x1, waiting for transfers between devices, local(): gathered = lax.all_gather(both, 'col', axis=0, tiled=True)  31.3 us
    dot_general x4, matrix products, contract_rows(): lax.dot_general(left, right, (((0,), (0,)), ((), ())), precision=precisio...  24.4 us
  transfers between devices with their start and end apart: 5, of which 4 were waited for; matrix products, arithmetic and copies ran while one was open for 2% of the time, Pallas kernels for 0%

commit v1 on v0

--- a/solution.py
+++ b/solution.py
@@ -92,16 +92,19 @@
     resident_two = resident[:, width:]
     inverse_one = -product[:, :width] * result_mask_one
     inverse_two = -(product[:, width:] + matmul(inverse_one, panel_above)) * result_mask_two
-    sums = lax.psum(
-        jnp.concatenate(
-            [
-                contract_rows(resident_one, inverse_one),
-                contract_rows(inverse_one, resident_two),
-                contract_rows(resident_two, inverse_two),
-            ],
-            axis=1,
+    sums = jnp.sum(
+        lax.all_gather(
+            jnp.concatenate(
+                [
+                    contract_rows(resident_one, inverse_one),
+                    contract_rows(inverse_one, resident_two),
+                    contract_rows(resident_two, inverse_two),
+                ],
+                axis=1,
+            ),
+            ("row", "col"),
         ),
-        ("row", "col"),
+        axis=0,
     )
     gram_one = sums[:, :width]
     cross_sum = sums[:, width : 2 * width]

time: 392 us -> 446 us (1.14)
  waiting for transfers between devices: 329 us -> 364 us
  local copies, waits for them, and re-layouts: 4 us -> 19.6 us
  other arithmetic: 5.13 us -> 11 us
    all_gather x0 -> x1, waiting for transfers between devices: none -> 155 us  [local(): lax.all_gather(jnp.concatenate([contract_rows(resident_one, inverse_one),...]
    psum x1 -> x0, waiting for transfers between devices: 127 us -> none  [local(): lax.psum(jnp.concatenate([contract_rows(resident_one, inverse_one), contr...]
    unnamed x20 -> x24, local copies, waits for them, and re-layouts: 2.86 us -> 18.4 us
    all_to_all x1, waiting for transfers between devices: 4.39 us -> 11.7 us  [deliver(): lax.all_to_all(outgoing, 'col', split_axis=0, concat_axis=0, tiled=True)]
    reduce_sum x0 -> x1, other arithmetic: none -> 5.83 us  [local(): jnp.sum(lax.all_gather(jnp.concatenate([contract_rows(resident_one, inver...]
  transfers between devices with their start and end apart: 5 -> 5, of which waited for: 4 -> 4; matrix products, arithmetic and copies ran while one was open for 2% -> 1% of each run, Pallas kernels for 0% -> 0%
where the time goes in v1:
time: 446 us; the launch traced here: 445 us
  waiting for transfers between devices  364 us (82%)
  matrix products  32 us (7%)
  local copies, waits for them, and re-layouts  19.6 us (4%)
  between operations  14.1 us (3%)
  other arithmetic  11 us (2%)
  starting transfers between devices  4.47 us (1%)
    reduce_scatter x1, waiting for transfers between devices, local(): lax.psum_scatter(contract_rows(ancestor_inverse, gathered, lax.Precision....  166 us
    all_gather x1, waiting for transfers between devices, local(): lax.all_gather(jnp.concatenate([contract_rows(resident_one, inverse_one),...  155 us
    all_gather x1, waiting for transfers between devices, local(): gathered = lax.all_gather(both, 'col', axis=0, tiled=True)  31.3 us
    dot_general x4, matrix products, contract_rows(): lax.dot_general(left, right, (((0,), (0,)), ((), ())), precision=precisio...  24.1 us
    unnamed x24, local copies, waits for them, and re-layouts  18.4 us
    all_to_all x1, waiting for transfers between devices, deliver(): lax.all_to_all(outgoing, 'col', split_axis=0, concat_axis=0, tiled=True)  11.7 us
  transfers between devices with their start and end apart: 5, of which 4 were waited for; matrix products, arithmetic and copies ran while one was open for 1% of the time, Pallas kernels for 0%

profile of v1, /device:TPU:0, one launch (start us, length us, event | category | flops | bytes accessed | tf_op | source)
XLA Modules:
  0.0 445.2 jit_solution(14361510297091302747)
XLA Ops:
  7.2 0.0 copy-start
  7.2 0.0 copy-start.6
  7.2 0.0 copy-start.7
  7.2 0.0 all-gather.4.cloned.1.call-start
  7.3 0.9 add_select_fusion.1
  8.2 0.8 add_select_fusion.3
  9.0 1.4 fusion.15
  10.4 1.3 fusion.12
  11.7 0.1 fusion.36
  11.8 0.0 copy-done.6
  11.8 0.1 broadcast_multiply_fusion
  11.9 0.0 copy-done.7
  11.9 0.1 broadcast_multiply_fusion.1
  12.0 1.0 pad_maximum_fusion
  13.0 0.0 all-gather.4.cloned.1.call-update
  13.0 0.0 reduce-scatter.2.cloned.1.call-start
  13.1 31.3 %all-gather.4.cloned.1.call-done = f32[1536,512]{1,0:T(8,128)} async-done(((f32[384,512]{1,0:T(8,128)}), f32[1536,512]{1,0:T(8,128)}) %all-gather.4.cloned.1.call-update) | async-done | bytes 3145744 | tf_op jit(solution)/shard_map/all_gather | solution.py:82
  44.4 22.1 %convolution_bitcast_fusion = f32[3072,512]{0,1:T(8,128)} fusion(f32[1536,512]{1,0:T(8,128)} %all-gather.4.cloned.1.call-done, f32[1536,3072]{1,0:T(8,128)} %param.9), kind=kOutput, calls=%fused_computation.3 | convolution fusion | flops 14495514624 | bytes 28311552 | tf_op jit(solution)/shard_map/dot_general | solution.py:14
  66.5 0.0 copy-start.1
  66.5 0.0 reduce-scatter.2.cloned.1.call-update
  66.6 0.0 copy-start.8
  66.6 0.0 all-gather.6.cloned.1.call-start
  66.6 1.0 copy-done.1
  67.7 0.7 collective-permute-start
  68.4 166.4 %reduce-scatter.2.cloned.1.call-done = f32[384,512]{0,1:T(8,128)} async-done(((f32[3072,512]{0,1:T(8,128)}), f32[384,512]{0,1:T(8,128)}) %reduce-scatter.2.cloned.1.call-update) | async-done | bytes 786448 | tf_op jit(solution)/shard_map/reduce_scatter | solution.py:85
  234.8 1.0 fusion.21
  235.8 0.0 collective-permute-done
  235.8 0.6 fusion.19
  236.4 0.8 fusion.24
  237.2 0.0 copy-done
  237.2 1.6 fusion.7
  238.9 0.6 fusion.22
  239.5 1.0 pad_maximum_fusion.1
  240.5 0.0 all-gather.6.cloned.1.call-update
  240.5 0.0 copy-done.8
  240.6 0.2 reduce_window_sum.11
  240.8 0.2 copy.38
  240.9 0.7 fusion.16
  241.6 0.9 copy.40
  242.5 3.7 all-to-all-start
  246.2 0.9 copy.41
  247.1 11.7 %all-to-all-done = f32[4,2,64,256]{3,2,1,0:T(8,128)S(1)} async-done(((f32[4,2,64,256]{3,2,1,0:T(8,128)}), f32[4,2,64,256]{3,2,1,0:T(8,128)S(1)}, u32[]{:S(2)}, u32[]{:S(2)}) %all-to-all-start) | async-done | bytes 524320 | tf_op jit(solution)/shard_map/all_to_all | solution.py:51
  258.8 154.6 %all-gather.6.cloned.1.call-done = f32[8192,768]{0,1:T(8,128)} async-done(((f32[256,768]{0,1:T(8,128)}), f32[8192,768]{0,1:T(8,128)}) %all-gather.6.cloned.1.call-update) | async-done | bytes 25165840 | tf_op jit(solution)/shard_map/all_gather | solution.py:96
  413.4 15.2 %copy.48 = f32[96,8,32,256]{3,2,1,0:T(8,128)S(1)} copy(f32[96,8,32,256]{3,1,2,0:T(8,128)} %bitcast.41) | data formatting | bytes 50331648
  428.6 0.0 copy-start.2
  428.6 5.8 %bitcast_reduce_fusion = f32[256,768]{0,1:T(8,128)S(1)} fusion(f32[96,8,32,256]{3,2,1,0:T(8,128)S(1)} %copy.48), kind=kLoop, calls=%fused_computation | loop fusion | flops 6094848 | bytes 25952256 | tf_op jit(solution)/shard_map/reduce_sum | solution.py:95
  434.4 0.0 copy-start.3
  434.4 0.1 fusion.35
  434.5 0.1 copy.45
  434.6 0.1 copy.46
  434.8 0.1 copy.47
  434.9 0.0 copy-done.2
  434.9 0.6 convolution_subtract_fusion.1
  435.5 0.0 copy-start.4
  435.5 0.4 fusion.9
  435.9 0.0 copy-done.3
  435.9 0.0 copy-start.5
  436.0 0.6 convolution_subtract_fusion
  436.6 1.3 fusion.8
  437.9 0.8 copy.54
  438.7 0.0 copy-done.4
  438.7 0.0 copy-done.5
  (4 shorter events, 0.0 us)
Async XLA Ops:
  7.2 230.1 %copy-start = (f32[256,256]{1,0:T(8,128)S(1)}, f32[256,256]{1,0:T(8,128)}, u32[]{:S(2)}) copy-start(f32[256,256]{1,0:T(8,128)} %param.15) | copy-start | bytes 786436
  7.2 4.6 %copy-start.6 = (f32[384,256]{1,0:T(8,128)S(1)}, f32[384,256]{1,0:T(8,128)}, u32[]{:S(2)}) copy-start(f32[384,256]{1,0:T(8,128)} %param.13) | copy-start | bytes 1179652
  7.2 4.7 %copy-start.7 = (f32[384,256]{1,0:T(8,128)S(1)}, f32[384,256]{1,0:T(8,128)}, u32[]{:S(2)}) copy-start(f32[384,256]{1,0:T(8,128)} %param.10) | copy-start | bytes 1179652
  7.2 37.2 %all-gather.4.cloned.1.call-start = ((), (), s32[]{:S(2)}) async-start(), calls=%async_computation.2 | async-start | bytes 3932160 | tf_op jit(solution)/shard_map/all_gather | solution.py:82
  13.0 221.7 %reduce-scatter.2.cloned.1.call-start = ((), (), s32[]{:S(2)}) async-start(), calls=%async_computation.3 | async-start | bytes 7077888 | tf_op jit(solution)/shard_map/reduce_scatter | solution.py:85
  66.5 1.1 copy-start.1
  66.6 174.0 %copy-start.8 = (s32[6,1]{0,1:T(1,128)S(1)}, s32[6,1]{0,1:T(1,128)}, u32[]{:S(2)}) copy-start(s32[6,1]{0,1:T(1,128)} %param.17) | copy-start | bytes 76
  66.6 346.8 %all-gather.6.cloned.1.call-start = ((), (), s32[]{:S(2)}) async-start(), calls=%async_computation.4 | async-start | bytes 25952256 | tf_op jit(solution)/shard_map/all_gather | solution.py:96
  67.7 168.1 %collective-permute-start = (f32[384,512]{1,0:T(8,128)S(1)}, f32[384,512]{1,0:T(8,128)S(1)}, u32[]{:S(2)}, u32[]{:S(2)}) collective-permute-start(f32[384,512]{1,0:T(8,128)S(1)} %copy-done.1), channel_id=1, source_target_pairs={{0,0},{1,4},{2,8},{3,12},{4,16},{5,20},{6,24},{7,28},{8,1},{9,5},{... | collective-permute-start | bytes 2359304 | tf_op jit(solution)/shard_map/ppermute | solution.py:84
  242.5 16.2 %all-to-all-start = ((f32[4,2,64,256]{3,2,1,0:T(8,128)}), f32[4,2,64,256]{3,2,1,0:T(8,128)S(1)}, u32[]{:S(2)}, u32[]{:S(2)}) async-start(f32[4,2,64,256]{3,2,1,0:T(8,128)} %copy.40), calls=%async_computation.1 | async-start | bytes 1048576 | tf_op jit(solution)/shard_map/all_to_all | solution.py:51
  428.6 6.3 %copy-start.2 = (f32[256,256]{1,0:T(8,128)S(1)}, f32[256,256]{1,0:T(8,128)}, u32[]{:S(2)}) copy-start(f32[256,256]{1,0:T(8,128)} %param.12) | copy-start | bytes 786436
  434.4 1.5 copy-start.3
  435.5 3.1 copy-start.4
  435.9 2.7 copy-start.5
Sparse Core Ops, SparseCore 0:
  13.2 31.2 all-gather.3
  66.7 168.0 reduce-scatter.1
  240.7 172.6 all-gather.5
